TPU v7x, 32 devices: a whole 2x2x4 slice. The times are simulated.
32 devices in a mesh: rep: 8 (over y, x, core), shard: 4 (over z).
Axes of the slice: x: 2, y: 2, z: 4, core: 2. Of those that a mesh axis runs over, the one named last changes fastest.
Arguments:
- inputs: bfloat16 [8, 4, 1104, 1024], P('rep', 'shard'), may hold values from -6 to 6
- counts: int32 [8], P('rep'), may hold values from 1 to 4, as said below
- ln1_gain: bfloat16 [1024], P('shard'), may hold values from 0.5 to 1.5
- ln1_shift: bfloat16 [1024], P('shard'), may hold values from -4 to 4
- w_qkv: bfloat16 [1024, 3072], P('shard'), may hold values from -0.1875 to 0.1875
- qv_bias: bfloat16 [2048], P('shard'), may hold values from -4 to 4
- w_out: bfloat16 [1024, 1024], P('shard'), may hold values from -0.75 to 0.75
- out_bias: bfloat16 [1024], P('shard'), may hold values from -4 to 4
- ln2_gain: bfloat16 [1024], P('shard'), may hold values from 0.5 to 1.5
- ln2_shift: bfloat16 [1024], P('shard'), may hold values from -4 to 4
- w_up: bfloat16 [1024, 4096], P('shard'), may hold values from -0.1875 to 0.1875
- up_bias: bfloat16 [4096], P('shard'), may hold values from -4 to 4
- w_down: bfloat16 [4096, 1024], P('shard'), may hold values from -0.09375 to 0.09375
- down_bias: bfloat16 [1024], P('shard'), may hold values from -4 to 4
- cotangent: bfloat16 [8, 4, 1104, 1024], P('rep', 'shard'), may hold values from -6 to 6
Outputs:
- output: bfloat16 [8, 4, 1104, 1024], P('rep', 'shard')
- input_grad: float32 [8, 4, 1104, 1024], P('rep', 'shard')
- grad_ln1_gain: float32 [1024], P('shard')
- grad_ln1_shift: float32 [1024], P('shard')
- grad_w_qkv: float32 [1024, 3072], P('shard')
- grad_qv_bias: float32 [2048], P('shard')
- grad_w_out: float32 [1024, 1024], P('shard')
- grad_out_bias: float32 [1024], P('shard')
- grad_ln2_gain: float32 [1024], P('shard')
- grad_ln2_shift: float32 [1024], P('shard')
- grad_w_up: float32 [1024, 4096], P('shard')
- grad_up_bias: float32 [4096], P('shard')
- grad_w_down: float32 [4096, 1024], P('shard')
- grad_down_bias: float32 [1024], P('shard')
Inputs may be any that keep to these rules, and one draw needn't show every extreme that they name: A group's live sequences occupy its slots 0 to counts - 1; some group has exactly 4 and some exactly 1.
All inputs are finite; a program needn't handle non-finite values.
Results may differ from a plain program's by a relative error of at most 0.018.
Values may be sent and summed in bfloat16 or wider, within the bound.
No kernel may reach another device: no remote copies, remote signals or barrier semaphores. Data moves between devices by JAX's collectives and lax.ppermute only.
A program may use at most 256 MiB of HBM per device.

v0:
```python
import jax
import jax.numpy as jnp
from jax import lax
from jax.sharding import PartitionSpec as P

HEADS = 16
HDIM = 64
eps = 1e-06
head_block = 4


def layer_norm(values, gain, shift):
    centre = values - jnp.mean(values, -1, keepdims=True)
    spread = jnp.mean(centre * centre, -1, keepdims=True)
    return centre * lax.rsqrt(spread + eps) * gain + shift


def gelu_exact(values):
    return jax.nn.gelu(values, approximate=False)


def matmul(left, right):
    return jnp.dot(left, right, preferred_element_type=jnp.float32)


def left_trans(left, right):
    return lax.dot_general(
        left, right, (((0,), (0,)), ((), ())), preferred_element_type=jnp.float32
    )


def right_trans(left, right):
    return lax.dot_general(
        left, right, (((1,), (1,)), ((), ())), preferred_element_type=jnp.float32
    )


def body(
    inputs,
    counts,
    ln1_gain,
    ln1_shift,
    w_qkv,
    qv_bias,
    w_out,
    out_bias,
    ln2_gain,
    ln2_shift,
    w_up,
    up_bias,
    w_down,
    down_bias,
    cotangent,
):
    gathered = (
        lax.all_gather(ln1_gain, "shard", axis=0, tiled=True),
        lax.all_gather(ln1_shift, "shard", axis=0, tiled=True),
        lax.all_gather(w_qkv, "shard", axis=0, tiled=True),
        lax.all_gather(qv_bias, "shard", axis=0, tiled=True),
        lax.all_gather(w_out, "shard", axis=0, tiled=True),
        lax.all_gather(out_bias, "shard", axis=0, tiled=True),
        lax.all_gather(ln2_gain, "shard", axis=0, tiled=True),
        lax.all_gather(ln2_shift, "shard", axis=0, tiled=True),
        lax.all_gather(w_up, "shard", axis=0, tiled=True),
        lax.all_gather(up_bias, "shard", axis=0, tiled=True),
        lax.all_gather(w_down, "shard", axis=0, tiled=True),
        lax.all_gather(down_bias, "shard", axis=0, tiled=True),
    )
    (
        full_g1,
        full_s1,
        full_qkv,
        full_qvb,
        full_wout,
        full_bout,
        full_g2,
        full_s2,
        full_wup,
        full_bup,
        full_wdown,
        full_bdown,
    ) = gathered
    slots = inputs.shape[1]
    seq_len = inputs.shape[2]
    width = inputs.shape[3]
    n_rows = slots * seq_len
    groups = HEADS // head_block
    scale = HDIM ** (-0.5)
    first_slot = lax.axis_index("shard") * slots
    alive = (jnp.arange(slots, dtype=jnp.int32) + first_slot < counts[0]).astype(jnp.float32)
    alive_rows = jnp.broadcast_to(alive[:, None], (slots, seq_len)).reshape(n_rows, 1)
    tokens = inputs.reshape(n_rows, width).astype(jnp.float32)
    hidden_one, norm_one_back = jax.vjp(
        layer_norm, tokens, full_g1.astype(jnp.float32), full_s1.astype(jnp.float32)
    )
    hidden_one_b = hidden_one.astype(jnp.bfloat16)
    projected = matmul(hidden_one_b, full_qkv)
    bias_f = full_qvb.astype(jnp.float32)
    queries_b = (projected[:, :width] + bias_f[:width]).astype(jnp.bfloat16)
    keys_b = projected[:, width : 2 * width].astype(jnp.bfloat16)
    values_b = (projected[:, 2 * width :] + bias_f[width:]).astype(jnp.bfloat16)

    def arrange(values):
        return values.reshape(slots, seq_len, groups, head_block, HDIM).transpose(2, 0, 1, 3, 4)

    def restore(values):
        return values.transpose(1, 2, 0, 3, 4).reshape(n_rows, width)

    query_groups = arrange(queries_b)
    key_groups = arrange(keys_b)
    value_groups = arrange(values_b)

    def forward_group(operands):
        query_part, key_part, value_part = operands
        scores = (
            jnp.einsum("cqhd,ckhd->chqk", query_part, key_part, preferred_element_type=jnp.float32)
            * scale
        )
        largest = jnp.max(scores, -1, keepdims=True)
        exponent = jnp.exp(scores - largest)
        denominator = jnp.sum(exponent, -1, keepdims=True)
        probs_b = (exponent / denominator).astype(jnp.bfloat16)
        mixed = jnp.einsum(
            "chqk,ckhd->cqhd", probs_b, value_part, preferred_element_type=jnp.float32
        )
        return (mixed, (largest + jnp.log(denominator))[..., 0])

    mixed_groups, log_totals = lax.map(forward_group, (query_groups, key_groups, value_groups))
    attended_b = restore(mixed_groups).astype(jnp.bfloat16)
    middle = tokens + matmul(attended_b, full_wout) + full_bout.astype(jnp.float32)
    hidden_two, norm_two_back = jax.vjp(
        layer_norm, middle, full_g2.astype(jnp.float32), full_s2.astype(jnp.float32)
    )
    hidden_two_b = hidden_two.astype(jnp.bfloat16)
    pre_act = matmul(hidden_two_b, full_wup) + full_bup.astype(jnp.float32)
    activated, gelu_back = jax.vjp(gelu_exact, pre_act)
    activated_b = activated.astype(jnp.bfloat16)
    result = middle + matmul(activated_b, full_wdown) + full_bdown.astype(jnp.float32)
    output = (alive_rows * result).astype(jnp.bfloat16).reshape(inputs.shape)
    again = (
        lax.all_gather(ln1_gain, "shard", axis=0, tiled=True),
        lax.all_gather(ln1_shift, "shard", axis=0, tiled=True),
        lax.all_gather(w_qkv, "shard", axis=0, tiled=True),
        lax.all_gather(qv_bias, "shard", axis=0, tiled=True),
        lax.all_gather(w_out, "shard", axis=0, tiled=True),
        lax.all_gather(out_bias, "shard", axis=0, tiled=True),
        lax.all_gather(ln2_gain, "shard", axis=0, tiled=True),
        lax.all_gather(ln2_shift, "shard", axis=0, tiled=True),
        lax.all_gather(w_up, "shard", axis=0, tiled=True),
        lax.all_gather(up_bias, "shard", axis=0, tiled=True),
        lax.all_gather(w_down, "shard", axis=0, tiled=True),
        lax.all_gather(down_bias, "shard", axis=0, tiled=True),
    )
    back_qkv = again[2]
    back_wout = again[4]
    back_wup = again[8]
    back_wdown = again[10]
    d_out = alive_rows * cotangent.reshape(n_rows, width).astype(jnp.float32)
    d_out_b = d_out.astype(jnp.bfloat16)
    grad_wdown = left_trans(activated_b, d_out_b)
    grad_bdown = jnp.sum(d_out, 0)
    d_act = right_trans(d_out_b, back_wdown)
    d_pre_b = gelu_back(d_act)[0].astype(jnp.bfloat16)
    grad_wup = left_trans(hidden_two_b, d_pre_b)
    grad_bup = jnp.sum(d_pre_b.astype(jnp.float32), 0)
    d_hidden_two = right_trans(d_pre_b, back_wup)
    d_mid_norm, grad_g2, grad_s2 = norm_two_back(d_hidden_two)
    d_mid = d_out + d_mid_norm
    d_proj_b = d_mid.astype(jnp.bfloat16)
    grad_wout = left_trans(attended_b, d_proj_b)
    grad_bout = jnp.sum(d_proj_b.astype(jnp.float32), 0)
    d_att_b = right_trans(d_proj_b, back_wout).astype(jnp.bfloat16)
    d_att_groups = arrange(d_att_b)

    def backward_group(operands):
        query_part, key_part, value_part, log_total, grad_part = operands
        scores = (
            jnp.einsum("cqhd,ckhd->chqk", query_part, key_part, preferred_element_type=jnp.float32)
            * scale
        )
        attn_probs = jnp.exp(scores - log_total[..., None])
        probs_b = attn_probs.astype(jnp.bfloat16)
        d_probs = jnp.einsum(
            "cqhd,ckhd->chqk", grad_part, value_part, preferred_element_type=jnp.float32
        )
        row_inner = jnp.sum(d_probs * attn_probs, -1, keepdims=True)
        d_scores_b = (attn_probs * (d_probs - row_inner)).astype(jnp.bfloat16)
        d_query = (
            jnp.einsum("chqk,ckhd->cqhd", d_scores_b, key_part, preferred_element_type=jnp.float32)
            * scale
        )
        d_key = (
            jnp.einsum(
                "chqk,cqhd->ckhd", d_scores_b, query_part, preferred_element_type=jnp.float32
            )
            * scale
        )
        d_value = jnp.einsum(
            "chqk,cqhd->ckhd", probs_b, grad_part, preferred_element_type=jnp.float32
        )
        return (d_query, d_key, d_value)

    d_query_groups, d_key_groups, d_value_groups = lax.map(
        backward_group, (query_groups, key_groups, value_groups, log_totals, d_att_groups)
    )
    d_qkv_b = jnp.concatenate(
        [restore(d_query_groups), restore(d_key_groups), restore(d_value_groups)], 1
    ).astype(jnp.bfloat16)
    grad_qkv = left_trans(hidden_one_b, d_qkv_b)
    column_sums = jnp.sum(d_qkv_b.astype(jnp.float32), 0)
    grad_qvb = jnp.concatenate([column_sums[:width], column_sums[2 * width :]])
    d_hidden_one = right_trans(d_qkv_b, back_qkv)
    d_in_norm, grad_g1, grad_s1 = norm_one_back(d_hidden_one)
    input_grad = (d_mid + d_in_norm).reshape(inputs.shape)
    owned = (
        lax.psum_scatter(
            grad_g1.astype(jnp.bfloat16), "shard", scatter_dimension=0, tiled=True
        ).astype(jnp.float32),
        lax.psum_scatter(
            grad_s1.astype(jnp.bfloat16), "shard", scatter_dimension=0, tiled=True
        ).astype(jnp.float32),
        lax.psum_scatter(
            grad_qkv.astype(jnp.bfloat16), "shard", scatter_dimension=0, tiled=True
        ).astype(jnp.float32),
        lax.psum_scatter(
            grad_qvb.astype(jnp.bfloat16), "shard", scatter_dimension=0, tiled=True
        ).astype(jnp.float32),
        lax.psum_scatter(
            grad_wout.astype(jnp.bfloat16), "shard", scatter_dimension=0, tiled=True
        ).astype(jnp.float32),
        lax.psum_scatter(
            grad_bout.astype(jnp.bfloat16), "shard", scatter_dimension=0, tiled=True
        ).astype(jnp.float32),
        lax.psum_scatter(
            grad_g2.astype(jnp.bfloat16), "shard", scatter_dimension=0, tiled=True
        ).astype(jnp.float32),
        lax.psum_scatter(
            grad_s2.astype(jnp.bfloat16), "shard", scatter_dimension=0, tiled=True
        ).astype(jnp.float32),
        lax.psum_scatter(
            grad_wup.astype(jnp.bfloat16), "shard", scatter_dimension=0, tiled=True
        ).astype(jnp.float32),
        lax.psum_scatter(
            grad_bup.astype(jnp.bfloat16), "shard", scatter_dimension=0, tiled=True
        ).astype(jnp.float32),
        lax.psum_scatter(
            grad_wdown.astype(jnp.bfloat16), "shard", scatter_dimension=0, tiled=True
        ).astype(jnp.float32),
        lax.psum_scatter(
            grad_bdown.astype(jnp.bfloat16), "shard", scatter_dimension=0, tiled=True
        ).astype(jnp.float32),
    )
    o_g1, o_s1, o_qkv, o_qvb, o_wout, o_bout, o_g2, o_s2, o_wup, o_bup, o_wdown, o_bdown = owned
    summed = (
        lax.psum(o_g1.astype(jnp.bfloat16), "rep").astype(jnp.float32),
        lax.psum(o_s1.astype(jnp.bfloat16), "rep").astype(jnp.float32),
        lax.psum(o_qkv.astype(jnp.bfloat16), "rep").astype(jnp.float32),
        lax.psum(o_qvb.astype(jnp.bfloat16), "rep").astype(jnp.float32),
        lax.psum(o_wout.astype(jnp.bfloat16), "rep").astype(jnp.float32),
        lax.psum(o_bout.astype(jnp.bfloat16), "rep").astype(jnp.float32),
        lax.psum(o_g2.astype(jnp.bfloat16), "rep").astype(jnp.float32),
        lax.psum(o_s2.astype(jnp.bfloat16), "rep").astype(jnp.float32),
        lax.psum(o_wup.astype(jnp.bfloat16), "rep").astype(jnp.float32),
        lax.psum(o_bup.astype(jnp.bfloat16), "rep").astype(jnp.float32),
        lax.psum(o_wdown.astype(jnp.bfloat16), "rep").astype(jnp.float32),
        lax.psum(o_bdown.astype(jnp.bfloat16), "rep").astype(jnp.float32),
    )
    return (
        output,
        input_grad,
        summed[0],
        summed[1],
        summed[2],
        summed[3],
        summed[4],
        summed[5],
        summed[6],
        summed[7],
        summed[8],
        summed[9],
        summed[10],
        summed[11],
    )


def solution(mesh):
    placed = (
        P("rep", "shard", None, None),
        P("rep"),
        P("shard"),
        P("shard"),
        P("shard", None),
        P("shard"),
        P("shard", None),
        P("shard"),
        P("shard"),
        P("shard"),
        P("shard", None),
        P("shard"),
        P("shard", None),
        P("shard"),
        P("rep", "shard", None, None),
    )
    return jax.shard_map(
        body,
        mesh=mesh,
        in_specs=placed,
        out_specs=(
            P("rep", "shard", None, None),
            P("rep", "shard", None, None),
            P("shard"),
            P("shard"),
            P("shard", None),
            P("shard"),
            P("shard", None),
            P("shard"),
            P("shard"),
            P("shard"),
            P("shard", None),
            P("shard"),
            P("shard", None),
            P("shard"),
        ),
        check_vma=False,
    )
```

profile of v0, /device:TPU:0, one launch (start us, length us, event | category | flops | bytes accessed | tf_op | source)
XLA Modules:
  0.0 1330.5 jit_solution(4466956774392505986)
XLA Ops:
  10.9 12.6 all-gather.5
  32.4 12.4 all-gather.3
  53.3 14.0 %all-gather = bf16[4,1,256]{2,1,0:T(2,128)(2,1)S(1)} all-gather(bf16[1,1,256]{2,1,0:T(2,128)(2,1)S(1)} %reshape.260), channel_id=1, replica_groups=mesh['rep'=8,'shard'=4] {'shard'}, dimensions={0}, use_global_device_ids=true | all-gather | bytes 2560 | tf_op jit(solution)/shard_map/all_gather | solution.py:56
  67.3 12.1 all-gather.2
  79.4 16.0 %all_gather.49 = bf16[4096]{0:T(1024)(128)(2,1)S(1)} all-gather(bf16[1024]{0:T(1024)(128)(2,1)S(1)} %copy-done.47), channel_id=1, replica_groups=mesh['rep'=8,'shard'=4] {'shard'}, dimensions={0}, use_global_device_ids=true | all-gather | bytes 10240 | tf_op jit(solution)/shard_map/all_gather | solution.py:65
  97.8 30.4 %all-gather.12.cloned.1.call-done = bf16[1024,3072]{1,0:T(8,128)(2,1)} async-done(((bf16[256,3072]{1,0:T(8,128)(2,1)}), bf16[1024,3072]{1,0:T(8,128)(2,1)}) %all-gather.12.cloned.1.call-update) | async-done | bytes 6291472 | tf_op jit(solution)/shard_map/all_gather | solution.py:58
  156.2 131.5 %while.26 = (s32[]{:T(128)}, bf16[4,1,1104,4,64]{2,4,3,1,0:T(8,128)(2,1)}, f32[4,1,4,1104]{3,2,1,0:T(4,128)}, bf16[4,1,1104,4,64]{2,4,3,1,0:T(8,128)(2,1)}, bf16...) while((s32[]{:T(128)}, bf16[4,1,1104,4,64]{2,4,3,1,0:T(8,128)(2,1)}, ...), condition=%wide.region_5.6_spmd, body=%wide.region_2.5_spmd.sunk | while | flops 1282190080 | bytes 62444376 | solution.py:128
  176.6 12.7 fusion.131
  297.9 26.0 %all-gather.16.cloned.1.call-done = bf16[1024,4096]{1,0:T(8,128)(2,1)} async-done(((bf16[256,4096]{1,0:T(8,128)(2,1)}), bf16[1024,4096]{1,0:T(8,128)(2,1)}) %all-gather.16.cloned.1.call-update) | async-done | bytes 8388624 | tf_op jit(solution)/shard_map/all_gather | solution.py:64
  323.9 54.4 %multiply_convert_fusion.1 = (bf16[1104,4096]{1,0:T(8,128)(2,1)}, f32[1104,4096]{1,0:T(8,128)}, f32[1104,4096]{1,0:T(8,128)}) fusion(f32[4096]{0:T(1024)S(1)} %copy-done.39, bf16[1024,4096]{1,0:T(8,128)(2,1)} %all-gather.16.cloned.1.call-done, f32[1104,1024]{1,0:T(8,128)} %copy-done.8, f32[1024]{0:T(1024)S(1)} %bitcast.254, f32[1024]{0:T(1024)S(1)} %bitcast.248, ...), kind=kOutput, calls=%fused_computation.56 | convolution fusion | flops 9565126656 | bytes 58163840 | tf_op jit(solution)/shard_map/dot_general | solution.py:23
  378.3 94.9 %all-gather.18.cloned.1.call-done = bf16[4096,1024]{1,0:T(8,128)(2,1)} async-done(((bf16[1024,1024]{1,0:T(8,128)(2,1)}), bf16[4096,1024]{1,0:T(8,128)(2,1)}) %all-gather.18.cloned.1.call-update) | async-done | bytes 8388624 | tf_op jit(solution)/shard_map/all_gather | solution.py:66
  473.2 25.4 %fusion.92 = (bf16[4096]{0:T(1024)(128)(2,1)}, bf16[1104,4096]{1,0:T(8,128)(2,1)}) fusion(f32[1104,4096]{1,0:T(8,128)} %get-tuple-element.193, f32[1104,4096]{1,0:T(8,128)} %get-tuple-element.206, bf16[4096,1024]{1,0:T(8,128)(2,1)} %all-gather.18.cloned.1.call-done, bf16[1,1,1104,1024]{3,2,1,0:T(8,128)(2,1)S(1)} %copy-done.6, f32[]{:T(128)} %bitcast.22), kind=kOutput, calls=%fused_computation.137 | convolution fusion | flops 9332240384 | bytes 55877636 | tf_op jit(solution)/shard_map/dot_general | solution.py:33
  498.6 18.1 %multiply_reduce_fusion.1 = (bf16[1024]{0:T(1024)(128)(2,1)}, f32[1104]{0:T(1024)S(1)}, bf16[1024]{0:T(1024)(128)(2,1)}, f32[1104,1024]{1,0:T(8,128)S(1)}) fusion(f32[1104,1024]{1,0:T(8,128)} %copy-done.8, f32[1104]{0:T(1024)S(1)} %fusion.76, f32[1104]{0:T(1024)S(1)} %broadcast_multiply_fusion, f32[1024]{0:T(1024)S(1)} %bitcast.249, ...), kind=kOutput, calls=%fused_computation.102 | convolution fusion | flops 9270064128 | bytes 26497984 | tf_op jit(solution)/shard_map/dot_general | solution.py:33
  538.8 243.8 %while.27 = (s32[]{:T(128)}, bf16[4,1,1104,4,64]{2,4,3,1,0:T(8,128)(2,1)}, bf16[4,1,1104,4,64]{2,4,3,1,0:T(8,128)(2,1)}, bf16[4,1,1104,4,64]{2,4,3,1,0:T(8,128)(...) while((s32[]{:T(128)}, ...), condition=%wide.region_12.13_spmd, body=%wide.region_10.12_spmd.sunk | while | flops 3159731968 | bytes 219023680 | solution.py:203
  560.7 17.6 %multiply_reduce_fusion.5 = (f32[4,1104]{1,0:T(4,128)S(1)}, f32[4,1104,1104]{1,2,0:T(8,128)}) fusion(f32[4,1104,1104]{1,2,0:T(8,128)} %fusion.140, bf16[4,1,1104,4,64]{2,4,3,1,0:T(8,128)(2,1)} %get-tuple-element.360, s32[]{:T(128)S(6)} %copy.89, bf16[4,1,1104,4,64]{2,4,3,1,0:T(8,128)(2,1)S(1)} %copy-done.5), kind=kOutput, calls=%fused_computation.20.clone.1 | convolution fusion | flops 633779904 | bytes 41048320 | tf_op jit(solution)/shard_map/while/body/eval_jaxpr/cqhd,ckhd->chqk/dot_general | solution.py:183
  578.4 13.5 %multiply_convert_fusion.3 = bf16[4,1104,1104]{1,2,0:T(8,128)(2,1)S(1)} fusion(f32[4,1104,1104]{1,2,0:T(8,128)} %fusion.140, f32[4,1104,1104]{1,2,0:T(8,128)} %get-tuple-element.309, f32[4,1104]{1,0:T(4,128)S(1)} %get-tuple-element.310), kind=kLoop, calls=%fused_computation.19.clone.1 | loop fusion | flops 14625792 | bytes 48770304 | tf_op jit(solution)/shard_map/while/body/eval_jaxpr/convert_element_type | solution.py:187
  621.6 17.5 %multiply_reduce_fusion.5 = (f32[4,1104]{1,0:T(4,128)S(1)}, f32[4,1104,1104]{1,2,0:T(8,128)}) fusion(f32[4,1104,1104]{1,2,0:T(8,128)} %fusion.140, bf16[4,1,1104,4,64]{2,4,3,1,0:T(8,128)(2,1)} %get-tuple-element.360, s32[]{:T(128)S(6)} %copy.89, bf16[4,1,1104,4,64]{2,4,3,1,0:T(8,128)(2,1)S(1)} %copy-done.5), kind=kOutput, calls=%fused_computation.20.clone.1 | convolution fusion | flops 633779904 | bytes 41048320 | tf_op jit(solution)/shard_map/while/body/eval_jaxpr/cqhd,ckhd->chqk/dot_general | solution.py:183
  639.2 13.5 %multiply_convert_fusion.3 = bf16[4,1104,1104]{1,2,0:T(8,128)(2,1)S(1)} fusion(f32[4,1104,1104]{1,2,0:T(8,128)} %fusion.140, f32[4,1104,1104]{1,2,0:T(8,128)} %get-tuple-element.309, f32[4,1104]{1,0:T(4,128)S(1)} %get-tuple-element.310), kind=kLoop, calls=%fused_computation.19.clone.1 | loop fusion | flops 14625792 | bytes 48770304 | tf_op jit(solution)/shard_map/while/body/eval_jaxpr/convert_element_type | solution.py:187
  682.5 17.5 %multiply_reduce_fusion.5 = (f32[4,1104]{1,0:T(4,128)S(1)}, f32[4,1104,1104]{1,2,0:T(8,128)}) fusion(f32[4,1104,1104]{1,2,0:T(8,128)} %fusion.140, bf16[4,1,1104,4,64]{2,4,3,1,0:T(8,128)(2,1)} %get-tuple-element.360, s32[]{:T(128)S(6)} %copy.89, bf16[4,1,1104,4,64]{2,4,3,1,0:T(8,128)(2,1)S(1)} %copy-done.5), kind=kOutput, calls=%fused_computation.20.clone.1 | convolution fusion | flops 633779904 | bytes 41048320 | tf_op jit(solution)/shard_map/while/body/eval_jaxpr/cqhd,ckhd->chqk/dot_general | solution.py:183
  700.0 13.5 %multiply_convert_fusion.3 = bf16[4,1104,1104]{1,2,0:T(8,128)(2,1)S(1)} fusion(f32[4,1104,1104]{1,2,0:T(8,128)} %fusion.140, f32[4,1104,1104]{1,2,0:T(8,128)} %get-tuple-element.309, f32[4,1104]{1,0:T(4,128)S(1)} %get-tuple-element.310), kind=kLoop, calls=%fused_computation.19.clone.1 | loop fusion | flops 14625792 | bytes 48770304 | tf_op jit(solution)/shard_map/while/body/eval_jaxpr/convert_element_type | solution.py:187
  743.3 17.5 %multiply_reduce_fusion.5 = (f32[4,1104]{1,0:T(4,128)S(1)}, f32[4,1104,1104]{1,2,0:T(8,128)}) fusion(f32[4,1104,1104]{1,2,0:T(8,128)} %fusion.140, bf16[4,1,1104,4,64]{2,4,3,1,0:T(8,128)(2,1)} %get-tuple-element.360, s32[]{:T(128)S(6)} %copy.89, bf16[4,1,1104,4,64]{2,4,3,1,0:T(8,128)(2,1)S(1)} %copy-done.5), kind=kOutput, calls=%fused_computation.20.clone.1 | convolution fusion | flops 633779904 | bytes 41048320 | tf_op jit(solution)/shard_map/while/body/eval_jaxpr/cqhd,ckhd->chqk/dot_general | solution.py:183
  760.9 13.5 %multiply_convert_fusion.3 = bf16[4,1104,1104]{1,2,0:T(8,128)(2,1)S(1)} fusion(f32[4,1104,1104]{1,2,0:T(8,128)} %fusion.140, f32[4,1104,1104]{1,2,0:T(8,128)} %get-tuple-element.309, f32[4,1104]{1,0:T(4,128)S(1)} %get-tuple-element.310), kind=kLoop, calls=%fused_computation.19.clone.1 | loop fusion | flops 14625792 | bytes 48770304 | tf_op jit(solution)/shard_map/while/body/eval_jaxpr/convert_element_type | solution.py:187
  782.6 15.3 %convolution_convert_fusion.2 = bf16[1024,3072]{1,0:T(8,128)(2,1)} fusion(bf16[1,1,1104,1024]{3,2,1,0:T(8,128)(2,1)} %param.19, f32[1024]{0:T(1024)S(1)} %bitcast.257, f32[1024]{0:T(1024)S(1)} %bitcast.244, f32[1104]{0:T(1024)S(1)} %copy-done.24, f32[1104]{0:T(1024)S(1)} %copy-done.22, bf16[1104,1024]{0,1:T(8,128)(2,1)} %bitcast.232, ...), kind=kOutput, calls=%fused_computation.75 | convolution fusion | flops 6976045056 | bytes 15352448 | tf_op jit(solution)/shard_map/dot_general | solution.py:27
  798.6 18.7 %convolution_convert_fusion.1 = bf16[1024,4096]{1,0:T(8,128)(2,1)} fusion(bf16[1104,4096]{1,0:T(8,128)(2,1)} %get-tuple-element.210, f32[1104,1024]{1,0:T(8,128)} %copy-done.8, f32[1024]{0:T(1024)S(1)} %bitcast.255, f32[1024]{0:T(1024)S(1)} %bitcast.251, f32[1104]{0:T(1024)S(1)} %copy-done.36, f32[1104]{0:T(1024)S(1)} %copy-done.26), kind=kOutput, calls=%fused_computation.71 | convolution fusion | flops 9270870016 | bytes 21971584 | tf_op jit(solution)/shard_map/dot_general | solution.py:27
  818.9 17.4 %convolution_convert_fusion = bf16[4096,1024]{1,0:T(8,128)(2,1)} fusion(bf16[1104,4096]{1,0:T(8,128)(2,1)} %get-tuple-element.192, bf16[1,1,1104,1024]{3,2,1,0:T(8,128)(2,1)S(1)} %copy-done.7, f32[]{:T(128)} %bitcast.22), kind=kOutput, calls=%fused_computation.70 | convolution fusion | flops 9268609024 | bytes 19693572 | tf_op jit(solution)/shard_map/dot_general | solution.py:27
  854.6 12.6 fusion.83
  872.0 22.2 %all-reduce.10 = (bf16[1024]{0:T(1024)(128)(2,1)S(1)}, bf16[1024]{0:T(1024)(128)(2,1)S(1)}, bf16[2048]{0:T(1024)(128)(2,1)S(1)}, bf16[1024]{0:T(1024)(128)(2,1)S...) all-reduce(bf16[1024]{0:T(1024)(128)(2,1)S(1)} %get-tuple-element.1, ...), channel_id=2, replica_groups=mesh['rep'=8,'shard'=4] {'shard'}, use_global_device_ids=true, to_apply=%region_16.17.clone | all-reduce | flops 12288 | bytes 49152
  894.8 12.5 all-reduce.8
  911.8 143.8 %reduce-scatter.9.cloned.1.call-done = bf16[256,4096]{1,0:T(8,128)(2,1)} async-done(((bf16[1024,4096]{1,0:T(8,128)(2,1)}), bf16[256,4096]{1,0:T(8,128)(2,1)}) %reduce-scatter.9.cloned.1.call-update) | async-done | bytes 2097168 | tf_op jit(solution)/shard_map/reduce_scatter | solution.py:240
  1055.6 147.7 %reduce-scatter.11.cloned.1.call-done = bf16[1024,1024]{1,0:T(8,128)(2,1)} async-done(((bf16[4096,1024]{1,0:T(8,128)(2,1)}), bf16[1024,1024]{1,0:T(8,128)(2,1)}) %reduce-scatter.11.cloned.1.call-update) | async-done | bytes 2097168 | tf_op jit(solution)/shard_map/reduce_scatter | solution.py:246
  1210.1 17.3 %fusion.72 = bf16[1,1,1104,1024]{3,2,1,0:T(8,128)(2,1)} fusion(f32[1104,1024]{1,0:T(8,128)} %copy-done.8, bf16[1104,4096]{1,0:T(8,128)(2,1)} %get-tuple-element.192, bf16[4096,1024]{1,0:T(8,128)(2,1)} %all-gather.18.cloned.1.call-done, f32[1024]{0:T(1024)S(1)} %bitcast.258, f32[]{:T(128)} %bitcast.22), kind=kOutput, calls=%fused_computation.111 | convolution fusion | flops 9265545216 | bytes 24219652 | tf_op jit(solution)/shard_map/dot_general | solution.py:23
  1227.4 85.5 %all-reduce.13.cloned.1.call-done = (bf16[256,3072]{1,0:T(8,128)(2,1)}, bf16[256,1024]{1,0:T(8,128)(2,1)}, bf16[256,4096]{1,0:T(8,128)(2,1)}, bf16[1024,1024]{1,0:T(8,128)(2,1)}) async-done(((bf16[256,3072]{1,0:T(8,128)(2,1)}, bf16[256,1024]{1,0:T(8,128)(2,1)}, bf16[256,4096]{1,0:T(8,128)(2,1)}, bf16[1024,1024]{1,0:T(8,128)(2,1)}), (bf16[256,3072]{1,0:T(8,128)(2,1)}, bf16[256,1024]{1,0:T(8,128)(2,1)}, ...) | async-done | bytes 6291472 | tf_op jit(solution)/shard_map/psum | solution.py:257
  (287 shorter events, 365.9 us)
Async XLA Ops:
  7.2 72.2 %copy-start.47 = (bf16[1024]{0:T(1024)(128)(2,1)S(1)}, bf16[1024]{0:T(1024)(128)(2,1)}, u32[]{:S(2)}) copy-start(bf16[1024]{0:T(1024)(128)(2,1)} %param.30) | copy-start | bytes 6148
  7.3 88.8 %copy-start.3 = (bf16[1,1,1104,1024]{3,2,1,0:T(8,128)(2,1)S(1)}, bf16[1,1,1104,1024]{3,2,1,0:T(8,128)(2,1)}, u32[]{:S(2)}) copy-start(bf16[1,1,1104,1024]{3,2,1,0:T(8,128)(2,1)} %param.19) | copy-start | bytes 6782980
  7.3 120.9 %all-gather.12.cloned.1.call-start = ((), (), s32[]{:S(2)}) async-start(), calls=%async_computation.4 | async-start | bytes 7864320 | tf_op jit(solution)/shard_map/all_gather | solution.py:58
  8.0 279.7 %all-gather.14.cloned.1.call-start = ((), (), s32[]{:S(2)}) async-start(), calls=%async_computation.5 | async-start | bytes 2621440 | tf_op jit(solution)/shard_map/all_gather | solution.py:60
  8.7 315.1 %all-gather.16.cloned.1.call-start = ((), (), s32[]{:S(2)}) async-start(), calls=%async_computation.6 | async-start | bytes 10485760 | tf_op jit(solution)/shard_map/all_gather | solution.py:64
  9.5 463.7 %all-gather.18.cloned.1.call-start = ((), (), s32[]{:S(2)}) async-start(), calls=%async_computation.7 | async-start | bytes 10485760 | tf_op jit(solution)/shard_map/all_gather | solution.py:66
  10.1 901.8 %reduce-scatter.7.cloned.1.call-start = ((), (), s32[]{:S(2)}) async-start(), calls=%async_computation.9 | async-start | bytes 2621440 | tf_op jit(solution)/shard_map/reduce_scatter | solution.py:228
  53.3 84.6 %copy-start.44 = (f32[4,1,256]{2,1,0:T(1,128)}, f32[4,1,256]{2,1,0:T(1,128)S(1)}, u32[]{:S(2)}) copy-start(f32[4,1,256]{2,1,0:T(1,128)S(1)} %convert_element_type.230) | copy-start | bytes 12292
  67.3 70.5 %copy-start.33 = (f32[4,1,256]{2,1,0:T(1,128)}, f32[4,1,256]{2,1,0:T(1,128)S(1)}, u32[]{:S(2)}) copy-start(f32[4,1,256]{2,1,0:T(1,128)S(1)} %convert_element_type.229) | copy-start | bytes 12292
  96.4 41.4 %copy-start.21 = (f32[1104]{0:T(1024)}, f32[1104]{0:T(1024)S(1)}, u32[]{:S(2)}) copy-start(f32[1104]{0:T(1024)S(1)} %broadcast_multiply_fusion.1) | copy-start | bytes 13252
  97.8 40.1 %copy-start.23 = (f32[1104]{0:T(1024)}, f32[1104]{0:T(1024)S(1)}, u32[]{:S(2)}) copy-start(f32[1104]{0:T(1024)S(1)} %fusion.75) | copy-start | bytes 13252
  156.2 131.5 %copy-start.46 = (f32[4,1,256]{2,1,0:T(1,128)S(1)}, f32[4,1,256]{2,1,0:T(1,128)}, u32[]{:S(2)}) copy-start(f32[4,1,256]{2,1,0:T(1,128)} %convert_element_type.232) | copy-start | bytes 12292
  294.6 29.3 %copy-start.37 = (f32[4,1,256]{2,1,0:T(1,128)S(1)}, f32[4,1,256]{2,1,0:T(1,128)}, u32[]{:S(2)}) copy-start(f32[4,1,256]{2,1,0:T(1,128)} %convert_element_type.233) | copy-start | bytes 12292
  294.6 29.3 %copy-start.39 = (f32[4096]{0:T(1024)S(1)}, f32[4096]{0:T(1024)}, u32[]{:S(2)}) copy-start(f32[4096]{0:T(1024)} %convert_element_type.198) | copy-start | bytes 49156
  294.6 29.3 %copy-start.42 = (f32[4,1,256]{2,1,0:T(1,128)S(1)}, f32[4,1,256]{2,1,0:T(1,128)}, u32[]{:S(2)}) copy-start(f32[4,1,256]{2,1,0:T(1,128)} %convert_element_type.234) | copy-start | bytes 12292
  294.6 222.1 %copy-start.25 = (f32[1104]{0:T(1024)}, f32[1104]{0:T(1024)S(1)}, u32[]{:S(2)}) copy-start(f32[1104]{0:T(1024)S(1)} %broadcast_multiply_fusion) | copy-start | bytes 13252
  297.9 218.8 %copy-start.35 = (f32[1104]{0:T(1024)}, f32[1104]{0:T(1024)S(1)}, u32[]{:S(2)}) copy-start(f32[1104]{0:T(1024)S(1)} %fusion.76) | copy-start | bytes 13252
  323.9 149.3 %copy-start.6 = (bf16[1,1,1104,1024]{3,2,1,0:T(8,128)(2,1)S(1)}, bf16[1,1,1104,1024]{3,2,1,0:T(8,128)(2,1)}, u32[]{:S(2)}) copy-start(bf16[1,1,1104,1024]{3,2,1,0:T(8,128)(2,1)} %param.33) | copy-start | bytes 6782980
  498.6 18.1 %copy-start.30 = (f32[1104]{0:T(1024)S(1)}, f32[1104]{0:T(1024)}, u32[]{:S(2)}) copy-start(f32[1104]{0:T(1024)} %copy-done.29) | copy-start | bytes 13252
  498.6 18.2 %copy-start.9 = (f32[1104,1024]{1,0:T(8,128)S(1)}, f32[1104,1024]{1,0:T(8,128)}, u32[]{:S(2)}) copy-start(f32[1104,1024]{1,0:T(8,128)} %copy-done.8) | copy-start | bytes 13565956
  526.0 385.8 %reduce-scatter.5.cloned.1.call-start = ((), (), s32[]{:S(2)}) async-start(), calls=%async_computation.8 | async-start | bytes 7864320 | tf_op jit(solution)/shard_map/reduce_scatter | solution.py:222
  538.8 243.8 %copy-start.22 = (f32[1104]{0:T(1024)S(1)}, f32[1104]{0:T(1024)}, u32[]{:S(2)}) copy-start(f32[1104]{0:T(1024)} %copy-done.21) | copy-start | bytes 13252
  538.8 243.8 %copy-start.24 = (f32[1104]{0:T(1024)S(1)}, f32[1104]{0:T(1024)}, u32[]{:S(2)}) copy-start(f32[1104]{0:T(1024)} %copy-done.23) | copy-start | bytes 13252
  538.8 243.8 %copy-start.34 = (f32[4,1,256]{2,1,0:T(1,128)S(1)}, f32[4,1,256]{2,1,0:T(1,128)}, u32[]{:S(2)}) copy-start(f32[4,1,256]{2,1,0:T(1,128)} %copy-done.33) | copy-start | bytes 12292
  538.8 243.8 %copy-start.45 = (f32[4,1,256]{2,1,0:T(1,128)S(1)}, f32[4,1,256]{2,1,0:T(1,128)}, u32[]{:S(2)}) copy-start(f32[4,1,256]{2,1,0:T(1,128)} %copy-done.44) | copy-start | bytes 12292
  560.7 17.6 %copy-start.12 = (bf16[4,1,1104,4,64]{2,4,3,1,0:T(8,128)(2,1)}, bf16[4,1,1104,4,64]{2,4,3,1,0:T(8,128)(2,1)S(1)}, u32[]{:S(2)}) copy-start(bf16[4,1,1104,4,64]{2,4,3,1,0:T(8,128)(2,1)S(1)} %fusion.143) | copy-start | bytes 6782980 | tf_op jit(solution)/shard_map/while
  621.6 17.6 %copy-start.12 = (bf16[4,1,1104,4,64]{2,4,3,1,0:T(8,128)(2,1)}, bf16[4,1,1104,4,64]{2,4,3,1,0:T(8,128)(2,1)S(1)}, u32[]{:S(2)}) copy-start(bf16[4,1,1104,4,64]{2,4,3,1,0:T(8,128)(2,1)S(1)} %fusion.143) | copy-start | bytes 6782980 | tf_op jit(solution)/shard_map/while
  682.5 17.6 %copy-start.12 = (bf16[4,1,1104,4,64]{2,4,3,1,0:T(8,128)(2,1)}, bf16[4,1,1104,4,64]{2,4,3,1,0:T(8,128)(2,1)S(1)}, u32[]{:S(2)}) copy-start(bf16[4,1,1104,4,64]{2,4,3,1,0:T(8,128)(2,1)S(1)} %fusion.143) | copy-start | bytes 6782980 | tf_op jit(solution)/shard_map/while
  797.9 257.7 %reduce-scatter.9.cloned.1.call-start = ((), (), s32[]{:S(2)}) async-start(), calls=%async_computation.10 | async-start | bytes 10485760 | tf_op jit(solution)/shard_map/reduce_scatter | solution.py:240
  817.3 386.0 %reduce-scatter.11.cloned.1.call-start = ((), (), s32[]{:S(2)}) async-start(), calls=%async_computation.11 | async-start | bytes 10485760 | tf_op jit(solution)/shard_map/reduce_scatter | solution.py:246
  836.3 476.6 %all-reduce.13.cloned.1.call-start = ((), (), s32[]{:S(2)}) async-start(), calls=%async_computation.12 | async-start | bytes 12582912 | tf_op jit(solution)/shard_map/psum | solution.py:257
  872.0 331.4 %copy-start.32 = (f32[1104]{0:T(1024)S(1)}, f32[1104]{0:T(1024)}, u32[]{:S(2)}) copy-start(f32[1104]{0:T(1024)} %copy-done.31) | copy-start | bytes 13252
  (56 other events, 299.8 us)
Sparse Core Ops, SparseCore 0:
  9.7 118.4 all-gather.11
  129.7 44.1 all-gather.13
  175.5 148.3 all-gather.15
  325.3 147.8 all-gather.17
  526.1 42.0 reduce-scatter.6
  798.1 110.0 reduce-scatter.4
  910.7 144.9 reduce-scatter.8
  1058.1 145.1 reduce-scatter.10
  1207.4 105.4 all-reduce.12
where the time goes:
time: 1340 us; the launch traced here: 1330 us
  waiting for transfers between devices  531 us (40%)
  matrix products  475 us (35%)
  other arithmetic  137 us (10%)
  blocking collectives  125 us (9%)
  local copies, waits for them, and re-layouts  42.8 us (3%)
  between operations  17.3 us (1%)
    reduce_scatter x1, waiting for transfers between devices, body(): lax.psum_scatter(grad_wdown.astype(jnp.bfloat16), 'shard', scatter_dimens...  148 us
    reduce_scatter x1, waiting for transfers between devices, body(): lax.psum_scatter(grad_wup.astype(jnp.bfloat16), 'shard', scatter_dimensio...  144 us
    all_gather x1, waiting for transfers between devices, body(): lax.all_gather(w_down, 'shard', axis=0, tiled=True)  94.9 us
    dot_general x4, matrix products, matmul(): return jnp.dot(left, right, preferred_element_type=jnp.float32)  88.1 us
    psum x1, waiting for transfers between devices, body(): lax.psum(o_qkv.astype(jnp.bfloat16), 'rep').astype(jnp.float32)  85.5 us
    dot_general x4, matrix products, backward_group(): jnp.einsum('cqhd,ckhd->chqk', grad_part, value_part, preferred_element_ty...  70.2 us
    dot_general x4, matrix products, right_trans(): lax.dot_general(left, right, (((1,), (1,)), ((), ())), preferred_element_...  61 us
    dot_general x4, matrix products, left_trans(): lax.dot_general(left, right, (((0,), (0,)), ((), ())), preferred_element_...  55.5 us
  transfers between devices with their start and end apart: 9, of which 6 were waited for; matrix products, arithmetic and copies ran while one was open for 43% of the time, Pallas kernels for 0%

commit v1 on v0

--- a/solution.py
+++ b/solution.py
@@ -254,7 +254,7 @@
     summed = (
         lax.psum(o_g1.astype(jnp.bfloat16), "rep").astype(jnp.float32),
         lax.psum(o_s1.astype(jnp.bfloat16), "rep").astype(jnp.float32),
-        lax.psum(o_qkv.astype(jnp.bfloat16), "rep").astype(jnp.float32),
+        jnp.sum(lax.all_gather(o_qkv.astype(jnp.bfloat16), "rep"), axis=0).astype(jnp.float32),
         lax.psum(o_qvb.astype(jnp.bfloat16), "rep").astype(jnp.float32),
         lax.psum(o_wout.astype(jnp.bfloat16), "rep").astype(jnp.float32),
         lax.psum(o_bout.astype(jnp.bfloat16), "rep").astype(jnp.float32),

time: 1340 us -> 1170 us (0.87)
  waiting for transfers between devices: 531 us -> 353 us
    reduce_scatter x1, waiting for transfers between devices: 144 us -> 0.02 us  [body(): lax.psum_scatter(grad_wup.astype(jnp.bfloat16), 'shard', scatter_dimensio...]
    reduce_scatter x1, waiting for transfers between devices: 148 us -> 23.1 us  [body(): lax.psum_scatter(grad_wdown.astype(jnp.bfloat16), 'shard', scatter_dimens...]
    reduce_scatter x1, waiting for transfers between devices: 0.01 us -> 114 us  [body(): lax.psum_scatter(grad_qkv.astype(jnp.bfloat16), 'shard', scatter_dimensio...]
    psum x1, waiting for transfers between devices: 85.5 us -> 0.01 us  [body(): lax.psum(o_wout.astype(jnp.bfloat16), 'rep').astype(jnp.float32)]
    all_gather x0 -> x1, waiting for transfers between devices: none -> 62.6 us  [body(): lax.all_gather(o_qkv.astype(jnp.bfloat16), 'rep')]
  transfers between devices with their start and end apart: 9 -> 10, of which waited for: 6 -> 6; matrix products, arithmetic and copies ran while one was open for 43% -> 51% of each run, Pallas kernels for 0% -> 0%
where the time goes in v1:
time: 1170 us; the launch traced here: 1160 us
  matrix products  477 us (41%)
  waiting for transfers between devices  353 us (30%)
  other arithmetic  145 us (12%)
  blocking collectives  122 us (10%)
  local copies, waits for them, and re-layouts  41.7 us (4%)
  between operations  17.9 us (2%)
    reduce_scatter x1, waiting for transfers between devices, body(): lax.psum_scatter(grad_qkv.astype(jnp.bfloat16), 'shard', scatter_dimensio...  114 us
    all_gather x1, waiting for transfers between devices, body(): lax.all_gather(w_down, 'shard', axis=0, tiled=True)  94.8 us
    dot_general x4, matrix products, matmul(): return jnp.dot(left, right, preferred_element_type=jnp.float32)  87.4 us
    dot_general x4, matrix products, backward_group(): jnp.einsum('cqhd,ckhd->chqk', grad_part, value_part, preferred_element_ty...  71.2 us
    all_gather x1, waiting for transfers between devices, body(): lax.all_gather(o_qkv.astype(jnp.bfloat16), 'rep')  62.6 us
    dot_general x4, matrix products, right_trans(): lax.dot_general(left, right, (((1,), (1,)), ((), ())), preferred_element_...  62.3 us
    dot_general x4, matrix products, left_trans(): lax.dot_general(left, right, (((0,), (0,)), ((), ())), preferred_element_...  55.1 us
    convert_element_type x4, other arithmetic, backward_group(): d_scores_b = (attn_probs * (d_probs - row_inner)).astype(jnp.bfloat16)  54.7 us
  transfers between devices with their start and end apart: 10, of which 6 were waited for; matrix products, arithmetic and copies ran while one was open for 51% of the time, Pallas kernels for 0%

profile of v1, /device:TPU:0, one launch (start us, length us, event | category | flops | bytes accessed | tf_op | source)
XLA Modules:
  0.0 1158.9 jit_solution(7479079227967921735)
XLA Ops:
  10.9 12.6 %all-gather.6 = bf16[4,1,256]{2,1,0:T(2,128)(2,1)S(1)} all-gather(bf16[1,1,256]{2,1,0:T(2,128)(2,1)S(1)} %reshape.271), channel_id=1, replica_groups=mesh['rep'=8,'shard'=4] {'shard'}, dimensions={0}, use_global_device_ids=true | all-gather | bytes 2560 | tf_op jit(solution)/shard_map/all_gather | solution.py:63
  32.4 12.4 %all-gather.4 = bf16[4,1,256]{2,1,0:T(2,128)(2,1)S(1)} all-gather(bf16[1,1,256]{2,1,0:T(2,128)(2,1)S(1)} %reshape.267), channel_id=1, replica_groups=mesh['rep'=8,'shard'=4] {'shard'}, dimensions={0}, use_global_device_ids=true | all-gather | bytes 2560 | tf_op jit(solution)/shard_map/all_gather | solution.py:61
  53.3 14.0 %all-gather.1 = bf16[4,1,256]{2,1,0:T(2,128)(2,1)S(1)} all-gather(bf16[1,1,256]{2,1,0:T(2,128)(2,1)S(1)} %reshape.261), channel_id=1, replica_groups=mesh['rep'=8,'shard'=4] {'shard'}, dimensions={0}, use_global_device_ids=true | all-gather | bytes 2560 | tf_op jit(solution)/shard_map/all_gather | solution.py:56
  67.3 12.1 %all-gather.3 = bf16[4,1,512]{2,1,0:T(2,128)(2,1)S(1)} all-gather(bf16[1,1,512]{2,1,0:T(2,128)(2,1)S(1)} %reshape.265), channel_id=1, replica_groups=mesh['rep'=8,'shard'=4] {'shard'}, dimensions={0}, use_global_device_ids=true | all-gather | bytes 5120 | tf_op jit(solution)/shard_map/all_gather | solution.py:59
  79.4 16.0 %all_gather.55 = bf16[4096]{0:T(1024)(128)(2,1)S(1)} all-gather(bf16[1024]{0:T(1024)(128)(2,1)S(1)} %copy-done.39), channel_id=1, replica_groups=mesh['rep'=8,'shard'=4] {'shard'}, dimensions={0}, use_global_device_ids=true | all-gather | bytes 10240 | tf_op jit(solution)/shard_map/all_gather | solution.py:65
  97.8 30.4 %all-gather.14.cloned.1.call-done = bf16[1024,3072]{1,0:T(8,128)(2,1)} async-done(((bf16[256,3072]{1,0:T(8,128)(2,1)}), bf16[1024,3072]{1,0:T(8,128)(2,1)}) %all-gather.14.cloned.1.call-update) | async-done | bytes 6291472 | tf_op jit(solution)/shard_map/all_gather | solution.py:58
  156.2 131.8 %while.26 = (s32[]{:T(128)}, bf16[4,1,1104,4,64]{2,4,3,1,0:T(8,128)(2,1)}, f32[4,1,4,1104]{3,2,1,0:T(4,128)}, bf16[4,1,1104,4,64]{2,4,3,1,0:T(8,128)(2,1)}, bf16...) while((s32[]{:T(128)}, bf16[4,1,1104,4,64]{2,4,3,1,0:T(8,128)(2,1)}, ...), condition=%wide.region_5.6_spmd, body=%wide.region_2.5_spmd.sunk | while | flops 1282190080 | bytes 62444376 | solution.py:128
  176.6 12.8 %fusion.131 = bf16[4,1,1104,4,64]{2,4,3,1,0:T(8,128)(2,1)} fusion(bf16[4,1,1104,4,64]{2,4,3,1,0:T(8,128)(2,1)} %get-tuple-element.318, s32[]{:T(128)S(6)} %copy.79, f32[4,1104,1104]{1,2,0:T(8,128)} %get-tuple-element.297, f32[4,1104]{1,0:T(4,128)S(1)} %fusion.130, f32[4,1104]{1,0:T(4,128)S(1)} %get-tuple-element.298, ...), kind=kOutput, calls=%fused_computation.6.clone.1 | convolution fusion | flops 638659584 | bytes 22154752 | tf_op jit(solution)/shard_map/while/body/eval_jaxpr/chqk,ckhd->cqhd/dot_general | solution.py:123
  298.2 25.7 %all-gather.18.cloned.1.call-done = bf16[1024,4096]{1,0:T(8,128)(2,1)} async-done(((bf16[256,4096]{1,0:T(8,128)(2,1)}), bf16[1024,4096]{1,0:T(8,128)(2,1)}) %all-gather.18.cloned.1.call-update) | async-done | bytes 8388624 | tf_op jit(solution)/shard_map/all_gather | solution.py:64
  323.9 54.5 %multiply_convert_fusion.1 = (bf16[1104,4096]{1,0:T(8,128)(2,1)}, f32[1104,4096]{1,0:T(8,128)}, f32[1104,4096]{1,0:T(8,128)}) fusion(f32[4096]{0:T(1024)S(1)} %copy-done.32, bf16[1024,4096]{1,0:T(8,128)(2,1)} %all-gather.18.cloned.1.call-done, f32[1104,1024]{1,0:T(8,128)} %copy-done.7, f32[1024]{0:T(1024)S(1)} %bitcast.258, f32[1024]{0:T(1024)S(1)} %bitcast.250, ...), kind=kOutput, calls=%fused_computation.56 | convolution fusion | flops 9565126656 | bytes 58163840 | tf_op jit(solution)/shard_map/dot_general | solution.py:23
  378.4 94.8 %all-gather.20.cloned.1.call-done = bf16[4096,1024]{1,0:T(8,128)(2,1)} async-done(((bf16[1024,1024]{1,0:T(8,128)(2,1)}), bf16[4096,1024]{1,0:T(8,128)(2,1)}) %all-gather.20.cloned.1.call-update) | async-done | bytes 8388624 | tf_op jit(solution)/shard_map/all_gather | solution.py:66
  473.2 25.1 %fusion.92 = (bf16[4096]{0:T(1024)(128)(2,1)}, bf16[1104,4096]{1,0:T(8,128)(2,1)}) fusion(f32[1104,4096]{1,0:T(8,128)} %get-tuple-element.192, f32[1104,4096]{1,0:T(8,128)} %get-tuple-element.205, bf16[4096,1024]{1,0:T(8,128)(2,1)} %all-gather.20.cloned.1.call-done, bf16[1,1,1104,1024]{3,2,1,0:T(8,128)(2,1)S(1)} %copy-done.6, f32[]{:T(128)} %bitcast.22), kind=kOutput, calls=%fused_computation.137 | convolution fusion | flops 9332240384 | bytes 55877636 | tf_op jit(solution)/shard_map/dot_general | solution.py:33
  498.3 18.1 %multiply_reduce_fusion.1 = (bf16[1024]{0:T(1024)(128)(2,1)}, f32[1104]{0:T(1024)S(1)}, bf16[1024]{0:T(1024)(128)(2,1)}, f32[1104,1024]{1,0:T(8,128)S(1)}) fusion(f32[1104,1024]{1,0:T(8,128)} %copy-done.7, f32[1104]{0:T(1024)S(1)} %fusion.76, f32[1104]{0:T(1024)S(1)} %broadcast_multiply_fusion, f32[1024]{0:T(1024)S(1)} %bitcast.251, ...), kind=kOutput, calls=%fused_computation.102 | convolution fusion | flops 9270064128 | bytes 26497984 | tf_op jit(solution)/shard_map/dot_general | solution.py:33
  526.0 17.9 %convolution_convert_fusion.1 = bf16[1024,4096]{1,0:T(8,128)(2,1)} fusion(bf16[1104,4096]{1,0:T(8,128)(2,1)} %get-tuple-element.209, f32[1104,1024]{1,0:T(8,128)} %copy-done.7, f32[1024]{0:T(1024)S(1)} %bitcast.259, f32[1024]{0:T(1024)S(1)} %bitcast.253, f32[1104]{0:T(1024)S(1)} %fusion.76, f32[1104]{0:T(1024)S(1)} %broadcast_multiply_fusion), kind=kOutput, calls=%fused_computation.71 | convolution fusion | flops 9270870016 | bytes 21971584 | tf_op jit(solution)/shard_map/dot_general | solution.py:27
  554.4 17.4 %convolution_convert_fusion = bf16[4096,1024]{1,0:T(8,128)(2,1)} fusion(bf16[1104,4096]{1,0:T(8,128)(2,1)} %get-tuple-element.191, bf16[1,1,1104,1024]{3,2,1,0:T(8,128)(2,1)S(1)} %copy-done.6, f32[]{:T(128)} %bitcast.22), kind=kOutput, calls=%fused_computation.70 | convolution fusion | flops 9268609024 | bytes 19693572 | tf_op jit(solution)/shard_map/dot_general | solution.py:27
  577.1 246.2 %while.27 = (s32[]{:T(128)}, bf16[4,1,1104,4,64]{2,4,3,1,0:T(8,128)(2,1)}, bf16[4,1,1104,4,64]{2,4,3,1,0:T(8,128)(2,1)}, bf16[4,1,1104,4,64]{2,4,3,1,0:T(8,128)(...) while((s32[]{:T(128)}, ...), condition=%wide.region_12.13_spmd, body=%wide.region_10.12_spmd.sunk | while | flops 3159731968 | bytes 219023680 | solution.py:203
  599.1 17.6 %multiply_reduce_fusion.5 = (f32[4,1104]{1,0:T(4,128)S(1)}, f32[4,1104,1104]{1,2,0:T(8,128)}) fusion(f32[4,1104,1104]{1,2,0:T(8,128)} %fusion.140, bf16[4,1,1104,4,64]{2,4,3,1,0:T(8,128)(2,1)} %get-tuple-element.359, s32[]{:T(128)S(6)} %copy.89, bf16[4,1,1104,4,64]{2,4,3,1,0:T(8,128)(2,1)S(1)} %copy-done.5), kind=kOutput, calls=%fused_computation.20.clone.1 | convolution fusion | flops 633779904 | bytes 41048320 | tf_op jit(solution)/shard_map/while/body/eval_jaxpr/cqhd,ckhd->chqk/dot_general | solution.py:183
  616.8 13.6 %multiply_convert_fusion.3 = bf16[4,1104,1104]{1,2,0:T(8,128)(2,1)S(1)} fusion(f32[4,1104,1104]{1,2,0:T(8,128)} %fusion.140, f32[4,1104,1104]{1,2,0:T(8,128)} %get-tuple-element.308, f32[4,1104]{1,0:T(4,128)S(1)} %get-tuple-element.309), kind=kLoop, calls=%fused_computation.19.clone.1 | loop fusion | flops 14625792 | bytes 48770304 | tf_op jit(solution)/shard_map/while/body/eval_jaxpr/convert_element_type | solution.py:187
  660.5 17.6 %multiply_reduce_fusion.5 = (f32[4,1104]{1,0:T(4,128)S(1)}, f32[4,1104,1104]{1,2,0:T(8,128)}) fusion(f32[4,1104,1104]{1,2,0:T(8,128)} %fusion.140, bf16[4,1,1104,4,64]{2,4,3,1,0:T(8,128)(2,1)} %get-tuple-element.359, s32[]{:T(128)S(6)} %copy.89, bf16[4,1,1104,4,64]{2,4,3,1,0:T(8,128)(2,1)S(1)} %copy-done.5), kind=kOutput, calls=%fused_computation.20.clone.1 | convolution fusion | flops 633779904 | bytes 41048320 | tf_op jit(solution)/shard_map/while/body/eval_jaxpr/cqhd,ckhd->chqk/dot_general | solution.py:183
  678.2 13.7 %multiply_convert_fusion.3 = bf16[4,1104,1104]{1,2,0:T(8,128)(2,1)S(1)} fusion(f32[4,1104,1104]{1,2,0:T(8,128)} %fusion.140, f32[4,1104,1104]{1,2,0:T(8,128)} %get-tuple-element.308, f32[4,1104]{1,0:T(4,128)S(1)} %get-tuple-element.309), kind=kLoop, calls=%fused_computation.19.clone.1 | loop fusion | flops 14625792 | bytes 48770304 | tf_op jit(solution)/shard_map/while/body/eval_jaxpr/convert_element_type | solution.py:187
  721.8 18.1 %multiply_reduce_fusion.5 = (f32[4,1104]{1,0:T(4,128)S(1)}, f32[4,1104,1104]{1,2,0:T(8,128)}) fusion(f32[4,1104,1104]{1,2,0:T(8,128)} %fusion.140, bf16[4,1,1104,4,64]{2,4,3,1,0:T(8,128)(2,1)} %get-tuple-element.359, s32[]{:T(128)S(6)} %copy.89, bf16[4,1,1104,4,64]{2,4,3,1,0:T(8,128)(2,1)S(1)} %copy-done.5), kind=kOutput, calls=%fused_computation.20.clone.1 | convolution fusion | flops 633779904 | bytes 41048320 | tf_op jit(solution)/shard_map/while/body/eval_jaxpr/cqhd,ckhd->chqk/dot_general | solution.py:183
  739.9 13.6 %multiply_convert_fusion.3 = bf16[4,1104,1104]{1,2,0:T(8,128)(2,1)S(1)} fusion(f32[4,1104,1104]{1,2,0:T(8,128)} %fusion.140, f32[4,1104,1104]{1,2,0:T(8,128)} %get-tuple-element.308, f32[4,1104]{1,0:T(4,128)S(1)} %get-tuple-element.309), kind=kLoop, calls=%fused_computation.19.clone.1 | loop fusion | flops 14625792 | bytes 48770304 | tf_op jit(solution)/shard_map/while/body/eval_jaxpr/convert_element_type | solution.py:187
  783.5 17.8 %multiply_reduce_fusion.5 = (f32[4,1104]{1,0:T(4,128)S(1)}, f32[4,1104,1104]{1,2,0:T(8,128)}) fusion(f32[4,1104,1104]{1,2,0:T(8,128)} %fusion.140, bf16[4,1,1104,4,64]{2,4,3,1,0:T(8,128)(2,1)} %get-tuple-element.359, s32[]{:T(128)S(6)} %copy.89, bf16[4,1,1104,4,64]{2,4,3,1,0:T(8,128)(2,1)S(1)} %copy-done.5), kind=kOutput, calls=%fused_computation.20.clone.1 | convolution fusion | flops 633779904 | bytes 41048320 | tf_op jit(solution)/shard_map/while/body/eval_jaxpr/cqhd,ckhd->chqk/dot_general | solution.py:183
  801.4 13.7 %multiply_convert_fusion.3 = bf16[4,1104,1104]{1,2,0:T(8,128)(2,1)S(1)} fusion(f32[4,1104,1104]{1,2,0:T(8,128)} %fusion.140, f32[4,1104,1104]{1,2,0:T(8,128)} %get-tuple-element.308, f32[4,1104]{1,0:T(4,128)S(1)} %get-tuple-element.309), kind=kLoop, calls=%fused_computation.19.clone.1 | loop fusion | flops 14625792 | bytes 48770304 | tf_op jit(solution)/shard_map/while/body/eval_jaxpr/convert_element_type | solution.py:187
  823.3 15.4 %convolution_convert_fusion.2 = bf16[1024,3072]{1,0:T(8,128)(2,1)} fusion(bf16[1,1,1104,1024]{3,2,1,0:T(8,128)(2,1)} %param.19, f32[1024]{0:T(1024)S(1)} %bitcast.257, f32[1024]{0:T(1024)S(1)} %bitcast.246, f32[1104]{0:T(1024)S(1)} %copy-done.22, f32[1104]{0:T(1024)S(1)} %copy-done.20, bf16[1104,1024]{0,1:T(8,128)(2,1)} %bitcast.234, ...), kind=kOutput, calls=%fused_computation.75 | convolution fusion | flops 6976045056 | bytes 15352448 | tf_op jit(solution)/shard_map/dot_general | solution.py:27
  838.9 23.1 %reduce-scatter.11.cloned.1.call-done = bf16[1024,1024]{1,0:T(8,128)(2,1)} async-done(((bf16[4096,1024]{1,0:T(8,128)(2,1)}), bf16[1024,1024]{1,0:T(8,128)(2,1)}) %reduce-scatter.11.cloned.1.call-update) | async-done | bytes 2097168 | tf_op jit(solution)/shard_map/reduce_scatter | solution.py:246
  862.1 113.8 %reduce-scatter.5.cloned.1.call-done = bf16[256,3072]{1,0:T(8,128)(2,1)} async-done(((bf16[1024,3072]{1,0:T(8,128)(2,1)}), bf16[256,3072]{1,0:T(8,128)(2,1)}) %reduce-scatter.5.cloned.1.call-update) | async-done | bytes 1572880 | tf_op jit(solution)/shard_map/reduce_scatter | solution.py:222
  995.6 12.8 %fusion.83 = (bf16[1024]{0:T(1024)(128)(2,1)S(1)}, f32[1104]{0:T(1024)S(1)}, f32[1104,1024]{1,0:T(8,128)S(1)}) fusion(f32[1024]{0:T(1024)S(1)} %bitcast.247, f32[1104]{0:T(1024)S(1)} %copy-done.20, bf16[1,1,1104,1024]{3,2,1,0:T(8,128)(2,1)S(1)} %copy-done.4, bf16[1024,3072]{1,0:T(8,128)(2,1)} %all-gather.14.cloned.1.call-done, ...), kind=kOutput, calls=%fused_computation.130 | convolution fusion | flops 6972897280 | bytes 19872384 | tf_op jit(solution)/shard_map/dot_general | solution.py:33
  1013.3 16.3 %all-reduce.10 = (bf16[1024]{0:T(1024)(128)(2,1)S(1)}, bf16[1024]{0:T(1024)(128)(2,1)S(1)}, bf16[2048]{0:T(1024)(128)(2,1)S(1)}, bf16[1024]{0:T(1024)(128)(2,1)S...) all-reduce(bf16[1024]{0:T(1024)(128)(2,1)S(1)} %get-tuple-element.1, ...), channel_id=3, replica_groups=mesh['rep'=8,'shard'=4] {'shard'}, use_global_device_ids=true, to_apply=%region_16.17.clone | all-reduce | flops 12288 | bytes 49152
  1030.1 12.6 %all-reduce.8 = (bf16[256]{0:T(256)(128)(2,1)S(1)}, bf16[256]{0:T(256)(128)(2,1)S(1)}, bf16[512]{0:T(512)(128)(2,1)S(1)}, bf16[256]{0:T(256)(128)(2,1)S(1)}, bf1...) all-reduce(bf16[256]{0:T(256)(128)(2,1)S(1)} %dynamic-slice.1, ...), channel_id=1, replica_groups=mesh['rep'=8,'shard'=4] {'rep'}, use_global_device_ids=true, to_apply=%region_17.18 | all-reduce | flops 3072 | bytes 12288 | tf_op jit(solution)/shard_map/psum | solution.py:255
  1054.4 16.4 %fusion.72 = bf16[1,1,1104,1024]{3,2,1,0:T(8,128)(2,1)} fusion(f32[1104,1024]{1,0:T(8,128)} %copy-done.7, bf16[1104,4096]{1,0:T(8,128)(2,1)} %get-tuple-element.191, bf16[4096,1024]{1,0:T(8,128)(2,1)} %all-gather.20.cloned.1.call-done, f32[1024]{0:T(1024)S(1)} %bitcast.260, f32[]{:T(128)} %bitcast.22), kind=kOutput, calls=%fused_computation.111 | convolution fusion | flops 9265545216 | bytes 24219652 | tf_op jit(solution)/shard_map/dot_general | solution.py:23
  1079.7 62.6 %all-gather.22.cloned.1.call-done = bf16[2048,3072]{1,0:T(8,128)(2,1)} async-done(((bf16[256,3072]{1,0:T(8,128)(2,1)}), bf16[2048,3072]{1,0:T(8,128)(2,1)}) %all-gather.22.cloned.1.call-update) | async-done | bytes 12582928 | tf_op jit(solution)/shard_map/all_gather | solution.py:257
  (275 shorter events, 376.8 us)
Async XLA Ops:
  7.2 72.2 %copy-start.39 = (bf16[1024]{0:T(1024)(128)(2,1)S(1)}, bf16[1024]{0:T(1024)(128)(2,1)}, u32[]{:S(2)}) copy-start(bf16[1024]{0:T(1024)(128)(2,1)} %param.30) | copy-start | bytes 6148
  7.3 88.8 %copy-start.3 = (bf16[1,1,1104,1024]{3,2,1,0:T(8,128)(2,1)S(1)}, bf16[1,1,1104,1024]{3,2,1,0:T(8,128)(2,1)}, u32[]{:S(2)}) copy-start(bf16[1,1,1104,1024]{3,2,1,0:T(8,128)(2,1)} %param.19) | copy-start | bytes 6782980
  7.3 120.9 %all-gather.14.cloned.1.call-start = ((), (), s32[]{:S(2)}) async-start(), calls=%async_computation.4 | async-start | bytes 7864320 | tf_op jit(solution)/shard_map/all_gather | solution.py:58
  8.0 280.0 %all-gather.16.cloned.1.call-start = ((), (), s32[]{:S(2)}) async-start(), calls=%async_computation.5 | async-start | bytes 2621440 | tf_op jit(solution)/shard_map/all_gather | solution.py:60
  8.7 315.1 %all-gather.18.cloned.1.call-start = ((), (), s32[]{:S(2)}) async-start(), calls=%async_computation.6 | async-start | bytes 10485760 | tf_op jit(solution)/shard_map/all_gather | solution.py:64
  9.5 463.7 %all-gather.20.cloned.1.call-start = ((), (), s32[]{:S(2)}) async-start(), calls=%async_computation.7 | async-start | bytes 10485760 | tf_op jit(solution)/shard_map/all_gather | solution.py:66
  10.1 828.8 %reduce-scatter.7.cloned.1.call-start = ((), (), s32[]{:S(2)}) async-start(), calls=%async_computation.9 | async-start | bytes 2621440 | tf_op jit(solution)/shard_map/reduce_scatter | solution.py:228
  53.3 84.6 %copy-start.35 = (f32[4,1,256]{2,1,0:T(1,128)}, f32[4,1,256]{2,1,0:T(1,128)S(1)}, u32[]{:S(2)}) copy-start(f32[4,1,256]{2,1,0:T(1,128)S(1)} %convert_element_type.232) | copy-start | bytes 12292
  67.3 70.5 %copy-start.29 = (f32[4,1,256]{2,1,0:T(1,128)}, f32[4,1,256]{2,1,0:T(1,128)S(1)}, u32[]{:S(2)}) copy-start(f32[4,1,256]{2,1,0:T(1,128)S(1)} %convert_element_type.231) | copy-start | bytes 12292
  96.4 41.4 %copy-start.19 = (f32[1104]{0:T(1024)}, f32[1104]{0:T(1024)S(1)}, u32[]{:S(2)}) copy-start(f32[1104]{0:T(1024)S(1)} %broadcast_multiply_fusion.1) | copy-start | bytes 13252
  97.8 40.1 %copy-start.21 = (f32[1104]{0:T(1024)}, f32[1104]{0:T(1024)S(1)}, u32[]{:S(2)}) copy-start(f32[1104]{0:T(1024)S(1)} %fusion.75) | copy-start | bytes 13252
  156.2 131.8 %copy-start.38 = (f32[4,1,256]{2,1,0:T(1,128)S(1)}, f32[4,1,256]{2,1,0:T(1,128)}, u32[]{:S(2)}) copy-start(f32[4,1,256]{2,1,0:T(1,128)} %convert_element_type.234) | copy-start | bytes 12292
  294.9 29.0 %copy-start.31 = (f32[4,1,256]{2,1,0:T(1,128)S(1)}, f32[4,1,256]{2,1,0:T(1,128)}, u32[]{:S(2)}) copy-start(f32[4,1,256]{2,1,0:T(1,128)} %convert_element_type.235) | copy-start | bytes 12292
  294.9 29.0 %copy-start.32 = (f32[4096]{0:T(1024)S(1)}, f32[4096]{0:T(1024)}, u32[]{:S(2)}) copy-start(f32[4096]{0:T(1024)} %convert_element_type.200) | copy-start | bytes 49156
  294.9 29.0 %copy-start.37 = (f32[4,1,256]{2,1,0:T(1,128)S(1)}, f32[4,1,256]{2,1,0:T(1,128)}, u32[]{:S(2)}) copy-start(f32[4,1,256]{2,1,0:T(1,128)} %convert_element_type.236) | copy-start | bytes 12292
  323.9 149.3 %copy-start.6 = (bf16[1,1,1104,1024]{3,2,1,0:T(8,128)(2,1)S(1)}, bf16[1,1,1104,1024]{3,2,1,0:T(8,128)(2,1)}, u32[]{:S(2)}) copy-start(bf16[1,1,1104,1024]{3,2,1,0:T(8,128)(2,1)} %param.33) | copy-start | bytes 6782980
  498.3 18.1 %copy-start.26 = (f32[1104]{0:T(1024)S(1)}, f32[1104]{0:T(1024)}, u32[]{:S(2)}) copy-start(f32[1104]{0:T(1024)} %copy-done.25) | copy-start | bytes 13252
  498.3 18.2 %copy-start.8 = (f32[1104,1024]{1,0:T(8,128)S(1)}, f32[1104,1024]{1,0:T(8,128)}, u32[]{:S(2)}) copy-start(f32[1104,1024]{1,0:T(8,128)} %copy-done.7) | copy-start | bytes 13565956
  525.9 313.0 %reduce-scatter.9.cloned.1.call-start = ((), (), s32[]{:S(2)}) async-start(), calls=%async_computation.10 | async-start | bytes 10485760 | tf_op jit(solution)/shard_map/reduce_scatter | solution.py:240
  543.9 318.1 %reduce-scatter.11.cloned.1.call-start = ((), (), s32[]{:S(2)}) async-start(), calls=%async_computation.11 | async-start | bytes 10485760 | tf_op jit(solution)/shard_map/reduce_scatter | solution.py:246
  571.8 404.1 %reduce-scatter.5.cloned.1.call-start = ((), (), s32[]{:S(2)}) async-start(), calls=%async_computation.8 | async-start | bytes 7864320 | tf_op jit(solution)/shard_map/reduce_scatter | solution.py:222
  577.1 246.2 %copy-start.20 = (f32[1104]{0:T(1024)S(1)}, f32[1104]{0:T(1024)}, u32[]{:S(2)}) copy-start(f32[1104]{0:T(1024)} %copy-done.19) | copy-start | bytes 13252
  577.1 246.2 %copy-start.22 = (f32[1104]{0:T(1024)S(1)}, f32[1104]{0:T(1024)}, u32[]{:S(2)}) copy-start(f32[1104]{0:T(1024)} %copy-done.21) | copy-start | bytes 13252
  577.1 246.2 %copy-start.30 = (f32[4,1,256]{2,1,0:T(1,128)S(1)}, f32[4,1,256]{2,1,0:T(1,128)}, u32[]{:S(2)}) copy-start(f32[4,1,256]{2,1,0:T(1,128)} %copy-done.29) | copy-start | bytes 12292
  577.1 246.3 %copy-start.36 = (f32[4,1,256]{2,1,0:T(1,128)S(1)}, f32[4,1,256]{2,1,0:T(1,128)}, u32[]{:S(2)}) copy-start(f32[4,1,256]{2,1,0:T(1,128)} %copy-done.35) | copy-start | bytes 12292
  721.8 18.1 %copy-start.11 = (bf16[4,1,1104,4,64]{2,4,3,1,0:T(8,128)(2,1)}, bf16[4,1,1104,4,64]{2,4,3,1,0:T(8,128)(2,1)S(1)}, u32[]{:S(2)}) copy-start(bf16[4,1,1104,4,64]{2,4,3,1,0:T(8,128)(2,1)S(1)} %fusion.143) | copy-start | bytes 6782980 | tf_op jit(solution)/shard_map/while
  783.5 17.9 %copy-start.11 = (bf16[4,1,1104,4,64]{2,4,3,1,0:T(8,128)(2,1)}, bf16[4,1,1104,4,64]{2,4,3,1,0:T(8,128)(2,1)S(1)}, u32[]{:S(2)}) copy-start(bf16[4,1,1104,4,64]{2,4,3,1,0:T(8,128)(2,1)S(1)} %fusion.143) | copy-start | bytes 6782980 | tf_op jit(solution)/shard_map/while
  838.8 137.2 %copy-start.49 = (u32[32]{0:T(128)S(1)}, u32[32]{0:T(128)}, u32[]{:S(2)}) copy-start(u32[32]{0:T(128)} %constant.133) | copy-start | bytes 388
  838.8 139.7 %copy-start.48 = (bf16[256]{0:T(256)(128)(2,1)S(1)}, bf16[256]{0:T(256)(128)(2,1)}, u32[]{:S(2)}) copy-start(bf16[256]{0:T(256)(128)(2,1)} %param.32) | copy-start | bytes 1540
  838.8 232.0 %all-reduce.13.cloned.1.call-start = ((), (), s32[]{:S(2)}) async-start(), calls=%async_computation.13 | async-start | bytes 9437184 | tf_op jit(solution)/shard_map/psum | solution.py:259
  862.1 280.2 %all-gather.22.cloned.1.call-start = ((), (), s32[]{:S(2)}) async-start(), calls=%async_computation.12 | async-start | bytes 14155776 | tf_op jit(solution)/shard_map/all_gather | solution.py:257
  1008.5 38.8 %copy-start.28 = (f32[1104]{0:T(1024)S(1)}, f32[1104]{0:T(1024)}, u32[]{:S(2)}) copy-start(f32[1104]{0:T(1024)} %copy-done.27) | copy-start | bytes 13252
  (49 other events, 305.2 us)
Sparse Core Ops, SparseCore 0:
  9.7 118.4 all-gather.13
  129.7 44.1 all-gather.15
  175.5 148.3 all-gather.17
  325.3 147.8 all-gather.19
  526.1 42.0 reduce-scatter.6
  570.5 143.7 reduce-scatter.8
  716.8 145.1 reduce-scatter.10
  864.5 111.4 reduce-scatter.4
  980.0 88.2 all-reduce.12
  1070.1 72.1 all-gather.21
